TPU v7x, 32 devices: a whole 2x2x4 slice. The times are simulated.
32 devices in a mesh: fsdp: 4 (over y, x), ctx: 4 (over z), tensor: 2 (over core).
Axes of the slice: x: 2, y: 2, z: 4, core: 2. Of those that a mesh axis runs over, the one named last changes fastest.
Arguments:
- layer_input: bfloat16 [8, 1024, 768], P(('fsdp', 'tensor'), 'ctx'), may hold values from -6 to 6
- cotangent: bfloat16 [8, 1024, 768], P(('fsdp', 'tensor'), 'ctx'), may hold values from -6 to 6
- segment_ids: int32 [8, 1024], P(('fsdp', 'tensor'), 'ctx'), may hold values from 0 to 5, as said below
- positions: int32 [8, 1024], P(('fsdp', 'tensor'), 'ctx'), may hold values from 0 to 1023, as said below
- query_key_value_weight: bfloat16 [768, 2304], P('fsdp'), may hold values from -0.21875 to 0.21875
- projection_matrix: bfloat16 [768, 768], P('fsdp'), may hold values from -0.875 to 0.875
- up_matrix: bfloat16 [768, 3072], P('fsdp', 'tensor'), may hold values from -0.21875 to 0.21875
- down_matrix: bfloat16 [3072, 768], P('tensor', 'fsdp'), may hold values from -0.109375 to 0.109375
- attn_gain: bfloat16 [768], P('fsdp'), may hold values from 0.5 to 1.5
- attn_shift: bfloat16 [768], P('fsdp'), may hold values from -3 to 3
- ffn_gain: bfloat16 [768], P('fsdp'), may hold values from 0.5 to 1.5
- ffn_shift: bfloat16 [768], P('fsdp'), may hold values from -3 to 3
- out_bias: bfloat16 [768], P('fsdp'), may hold values from -3 to 3
- up_projection_bias: bfloat16 [3072], P('fsdp'), may hold values from -3 to 3
Outputs:
- layer_output: bfloat16 [8, 1024, 768], P(('fsdp', 'tensor'), 'ctx')
- input_grad: float32 [8, 1024, 768], P(('fsdp', 'tensor'), 'ctx')
- qkv_grad: float32 [768, 2304], P('fsdp')
- proj_grad: float32 [768, 768], P('fsdp')
- up_grad: float32 [768, 3072], P('fsdp', 'tensor')
- down_grad: float32 [3072, 768], P('tensor', 'fsdp')
- attn_gain_grad: float32 [768], P('fsdp')
- attn_shift_grad: float32 [768], P('fsdp')
- ffn_gain_grad: float32 [768], P('fsdp')
- ffn_shift_grad: float32 [768], P('fsdp')
- out_bias_grad: float32 [768], P('fsdp')
- up_bias_grad: float32 [3072], P('fsdp')
Inputs may be any that keep to these rules, and one draw needn't show every extreme that they name: `segment_ids`: along each sequence the ids start at 0 and rise by one at each document's first token; every document has 200 to 1024 tokens, except the last one of a sequence, which the sequence's end may cut. `positions`: each document's tokens count 0, 1, 2, ... from its first token, which starts with the segment_ids' change.
All inputs are finite; a program needn't handle non-finite values.
Results may differ from a plain program's by a relative error of at most 0.018.
Values may be sent and summed in bfloat16 or wider, within the bound.
No kernel may reach another device: no remote copies, remote signals or barrier semaphores. Data moves between devices by JAX's collectives and lax.ppermute only.
A program may use at most 192 MiB of HBM per device.

v0:
```python
import math
import jax
import jax.numpy as jnp
from jax import lax
from jax.sharding import PartitionSpec as P

HEADS = 12
HEAD = 64
ROT = 16
FF = 3072
epsilon = 1e-05
masked_score = -1e30


def normalize(values):
    center = jnp.mean(values, axis=-1, keepdims=True)
    shifted = values - center
    spread = jnp.mean(shifted * shifted, axis=-1, keepdims=True)
    inverse = lax.rsqrt(spread + epsilon)
    return (shifted * inverse, inverse)


def norm_back(grad_hidden, normed, inverse, gain_vec):
    scaled = grad_hidden * gain_vec
    first_mean = jnp.mean(scaled, axis=-1, keepdims=True)
    second_mean = jnp.mean(scaled * normed, axis=-1, keepdims=True)
    return inverse * (scaled - first_mean - normed * second_mean)


def rotary_tables(positions):
    half_rot = ROT // 2
    frequency = 10000.0 ** (-(2.0 * jnp.arange(half_rot, dtype=jnp.float32)) / ROT)
    angles = positions.astype(jnp.float32)[..., None] * frequency
    return (jnp.cos(angles), jnp.sin(angles))


def rotate(fields, cosine, sine_tab):
    half_rot = ROT // 2
    first_half = fields[..., :half_rot]
    second = fields[..., half_rot:ROT]
    return jnp.concatenate(
        [
            first_half * cosine - second * sine_tab,
            second * cosine + first_half * sine_tab,
            fields[..., ROT:],
        ],
        axis=-1,
    )


def unrotate(fields, cosine, sine_tab):
    half_rot = ROT // 2
    first_half = fields[..., :half_rot]
    second = fields[..., half_rot:ROT]
    return jnp.concatenate(
        [
            first_half * cosine + second * sine_tab,
            second * cosine - first_half * sine_tab,
            fields[..., ROT:],
        ],
        axis=-1,
    )


def exact_gelu(values):
    return jax.nn.gelu(values, approximate=False)


def to_tokens(blocks):
    return lax.all_to_all(blocks, "ctx", split_axis=1, concat_axis=3, tiled=True)


def tensor_total(terms):
    return lax.psum_scatter(
        terms.astype(jnp.bfloat16), "tensor", scatter_dimension=0, tiled=True
    ).astype(jnp.float32)


def shards(
    layer_input,
    cotangent,
    segment_ids,
    positions,
    query_key_value_weight,
    projection_matrix,
    up_matrix,
    down_matrix,
    attn_gain,
    attn_shift,
    ffn_gain,
    ffn_shift,
    out_bias,
    up_projection_bias,
):
    ctx_size = lax.axis_size("ctx")
    tensor_size = lax.axis_size("tensor")
    seq_count, piece_len, model_width = layer_input.shape
    token_count = seq_count * piece_len
    ffn_share = FF // tensor_size
    (
        full_qkv,
        full_proj,
        up_share,
        down_share,
        gain_one,
        shift_one,
        gain_two,
        shift_two,
        bias_all,
        up_bias_all,
    ) = (
        lax.all_gather(query_key_value_weight, "fsdp", axis=0, tiled=True),
        lax.all_gather(projection_matrix, "fsdp", axis=0, tiled=True),
        lax.all_gather(up_matrix, "fsdp", axis=0, tiled=True),
        lax.all_gather(down_matrix, "fsdp", axis=1, tiled=True),
        lax.all_gather(attn_gain, "fsdp", axis=0, tiled=True),
        lax.all_gather(attn_shift, "fsdp", axis=0, tiled=True),
        lax.all_gather(ffn_gain, "fsdp", axis=0, tiled=True),
        lax.all_gather(ffn_shift, "fsdp", axis=0, tiled=True),
        lax.all_gather(out_bias, "fsdp", axis=0, tiled=True),
        lax.all_gather(up_projection_bias, "fsdp", axis=0, tiled=True),
    )
    gain_one = gain_one.astype(jnp.float32)
    shift_one = shift_one.astype(jnp.float32)
    gain_two = gain_two.astype(jnp.float32)
    shift_two = shift_two.astype(jnp.float32)
    up_bias_f = up_bias_all.astype(jnp.float32)
    inputs = layer_input.reshape(token_count, model_width).astype(jnp.float32)
    normed, inverse = normalize(inputs)
    first_hidden = (normed * gain_one + shift_one).astype(jnp.bfloat16)
    second_hidden = (normed * gain_two + shift_two).astype(jnp.bfloat16)
    projected_output = jnp.dot(first_hidden, full_qkv, preferred_element_type=jnp.float32).reshape(
        token_count, 3, HEADS, HEAD
    )
    cosine, sine_tab = rotary_tables(positions.reshape(token_count))
    cosine = cosine[:, None, :]
    sine_tab = sine_tab[:, None, :]
    query_tok = rotate(projected_output[:, 0], cosine, sine_tab).astype(jnp.bfloat16)
    key_tok = rotate(projected_output[:, 1], cosine, sine_tab).astype(jnp.bfloat16)
    value_tok = projected_output[:, 2].astype(jnp.bfloat16)
    packed = jnp.stack([query_tok, key_tok, value_tok], axis=1).reshape(
        seq_count, piece_len, 3, HEADS, HEAD
    )
    seg_send = jnp.broadcast_to(
        segment_ids.astype(jnp.bfloat16)[:, :, None, None], (seq_count, piece_len, 1, ctx_size)
    )
    headed, seg_heads = (
        lax.all_to_all(packed, "ctx", split_axis=3, concat_axis=1, tiled=True),
        lax.all_to_all(seg_send, "ctx", split_axis=3, concat_axis=1, tiled=True),
    )
    seq_len = headed.shape[1]
    seg_full = seg_heads.reshape(seq_count, seq_len)
    query_all = headed[:, :, 0]
    key_all = headed[:, :, 1]
    value_all = headed[:, :, 2]
    block_rows = min(512, seq_len)
    scale = math.sqrt(HEAD)

    def block_scores(row_start):
        query_block = lax.dynamic_slice_in_dim(query_all, row_start, block_rows, 1)
        scores = (
            jnp.einsum("sqhe,skhe->shqk", query_block, key_all, preferred_element_type=jnp.float32)
            / scale
        )
        row_ids = row_start + jnp.arange(block_rows)
        col_ids = jnp.arange(seq_len)
        causal = col_ids[None, :] <= row_ids[:, None]
        seg_rows = lax.dynamic_slice_in_dim(seg_full, row_start, block_rows, 1)
        same_doc = seg_rows[:, :, None] == seg_full[:, None, :]
        allowed = (same_doc & causal[None])[:, None]
        return (query_block, jnp.where(allowed, scores, masked_score), allowed)

    context_parts = []
    log_totals = []
    for row_start in range(0, seq_len, block_rows):
        query_block, masked, allowed = block_scores(row_start)
        row_peak = jnp.max(masked, axis=-1, keepdims=True)
        exp_terms = jnp.exp(masked - row_peak)
        row_total = jnp.sum(exp_terms, axis=-1, keepdims=True)
        attn_probs = (exp_terms / row_total).astype(jnp.bfloat16)
        log_totals.append(row_peak + jnp.log(row_total))
        context_parts.append(
            jnp.einsum(
                "shqk,skhe->sqhe", attn_probs, value_all, preferred_element_type=jnp.float32
            ).astype(jnp.bfloat16)
        )
    context_rows = jnp.concatenate(context_parts, axis=1)
    context_tok = to_tokens(context_rows[:, :, None]).reshape(token_count, model_width)
    attention_branch = jnp.dot(context_tok, full_proj, preferred_element_type=jnp.float32)
    grad_bf = cotangent.reshape(token_count, model_width)
    rows_two, rows_grad = (
        lax.all_gather(
            second_hidden.reshape(seq_count, piece_len, model_width), "tensor", axis=0, tiled=True
        ),
        lax.all_gather(cotangent, "tensor", axis=0, tiled=True),
    )
    rows_two = rows_two.reshape(-1, model_width)
    rows_grad = rows_grad.reshape(-1, model_width)
    offset = lax.axis_index("tensor") * ffn_share
    bias_share = lax.dynamic_slice_in_dim(up_bias_f, offset, ffn_share, 0)
    preactivation = jnp.dot(rows_two, up_share, preferred_element_type=jnp.float32) + bias_share
    activated_hidden, gelu_back = jax.vjp(exact_gelu, preactivation)
    act_bf = activated_hidden.astype(jnp.bfloat16)
    feed_part = jnp.dot(act_bf, down_share, preferred_element_type=jnp.float32).reshape(
        tensor_size * seq_count, piece_len, model_width
    )
    feedforward_output = tensor_total(feed_part).reshape(token_count, model_width)
    grad_act = jnp.einsum("td,fd->tf", rows_grad, down_share, preferred_element_type=jnp.float32)
    grad_pre = gelu_back(grad_act)[0].astype(jnp.bfloat16)
    back_part = jnp.einsum(
        "tf,df->td", grad_pre, up_share, preferred_element_type=jnp.float32
    ).reshape(tensor_size * seq_count, piece_len, model_width)
    grad_two = tensor_total(back_part).reshape(token_count, model_width)
    up_part = jnp.einsum("tf,td->fd", grad_pre, rows_two, preferred_element_type=jnp.float32)
    down_part = jnp.einsum("tf,td->fd", act_bf, rows_grad, preferred_element_type=jnp.float32)
    ffn_grad = jnp.stack([up_part, down_part], axis=1)
    up_bias_grad = lax.dynamic_update_slice_in_dim(
        jnp.zeros((FF,), jnp.float32), jnp.sum(grad_pre, axis=0, dtype=jnp.float32), offset, 0
    )
    output = inputs + attention_branch + feedforward_output + bias_all.astype(jnp.float32)
    layer_output = output.astype(jnp.bfloat16).reshape(seq_count, piece_len, model_width)
    grad_context = jnp.einsum(
        "td,cd->tc", grad_bf, full_proj, preferred_element_type=jnp.float32
    ).astype(jnp.bfloat16)
    grad_heads = lax.all_to_all(
        grad_context.reshape(seq_count, piece_len, 1, HEADS, HEAD),
        "ctx",
        split_axis=3,
        concat_axis=1,
        tiled=True,
    )[:, :, 0]
    grad_key = jnp.zeros(key_all.shape, jnp.float32)
    grad_value = jnp.zeros(value_all.shape, jnp.float32)
    query_parts = []
    for part_index, row_start in enumerate(range(0, seq_len, block_rows)):
        query_block, masked, allowed = block_scores(row_start)
        grad_block = lax.dynamic_slice_in_dim(grad_heads, row_start, block_rows, 1)
        full_probs = jnp.where(allowed, jnp.exp(masked - log_totals[part_index]), 0.0)
        grad_probs = jnp.einsum(
            "sqhe,skhe->shqk", grad_block, value_all, preferred_element_type=jnp.float32
        )
        row_delta = jnp.sum(full_probs * grad_probs, axis=-1, keepdims=True)
        grad_scores = (full_probs * (grad_probs - row_delta)).astype(jnp.bfloat16)
        query_parts.append(
            jnp.einsum("shqk,skhe->sqhe", grad_scores, key_all, preferred_element_type=jnp.float32)
            / scale
        )
        grad_key = (
            grad_key
            + jnp.einsum(
                "shqk,sqhe->skhe", grad_scores, query_block, preferred_element_type=jnp.float32
            )
            / scale
        )
        grad_value = grad_value + jnp.einsum(
            "shqk,sqhe->skhe",
            full_probs.astype(jnp.bfloat16),
            grad_block,
            preferred_element_type=jnp.float32,
        )
    grad_query = jnp.concatenate(query_parts, axis=1)
    grad_stack = jnp.stack([grad_query, grad_key, grad_value], axis=2).astype(jnp.bfloat16)
    grad_tok = to_tokens(grad_stack).reshape(token_count, 3, HEADS, HEAD).astype(jnp.float32)
    grad_proj = jnp.stack(
        [
            unrotate(grad_tok[:, 0], cosine, sine_tab),
            unrotate(grad_tok[:, 1], cosine, sine_tab),
            grad_tok[:, 2],
        ],
        axis=1,
    )
    grad_proj = grad_proj.reshape(token_count, 3 * model_width).astype(jnp.bfloat16)
    grad_one = jnp.einsum("tc,dc->td", grad_proj, full_qkv, preferred_element_type=jnp.float32)
    cot_float = grad_bf.astype(jnp.float32)
    input_grad = (
        cot_float
        + norm_back(grad_one, normed, inverse, gain_one)
        + norm_back(grad_two, normed, inverse, gain_two)
    )
    qkv_part = jnp.einsum("tr,tc->rc", first_hidden, grad_proj, preferred_element_type=jnp.float32)
    proj_part = jnp.einsum("tr,tc->rc", context_tok, grad_bf, preferred_element_type=jnp.float32)
    attn_grad = lax.psum_scatter(
        jnp.concatenate([qkv_part, proj_part], axis=1).astype(jnp.bfloat16),
        "fsdp",
        scatter_dimension=0,
        tiled=True,
    )
    small_grad = jnp.stack(
        [
            jnp.sum(grad_one * normed, axis=0),
            jnp.sum(grad_one, axis=0),
            jnp.sum(grad_two * normed, axis=0),
            jnp.sum(grad_two, axis=0),
            jnp.sum(cot_float, axis=0),
        ]
    )
    ffn_part, small_part, bias_part = (
        lax.psum_scatter(
            ffn_grad.astype(jnp.bfloat16), "fsdp", scatter_dimension=2, tiled=True
        ).astype(jnp.float32),
        lax.psum_scatter(
            small_grad.astype(jnp.bfloat16), "fsdp", scatter_dimension=1, tiled=True
        ).astype(jnp.float32),
        lax.psum_scatter(
            up_bias_grad.astype(jnp.bfloat16), "fsdp", scatter_dimension=0, tiled=True
        ).astype(jnp.float32),
    )
    attn_sum, small_sum, bias_sum = (
        lax.psum(attn_grad, ("ctx", "tensor")).astype(jnp.float32),
        lax.psum(small_part.astype(jnp.bfloat16), ("ctx", "tensor")).astype(jnp.float32),
        lax.psum(bias_part.astype(jnp.bfloat16), ("ctx", "tensor")).astype(jnp.float32),
    )
    ffn_sum = lax.psum(ffn_part.astype(jnp.bfloat16), "ctx").astype(jnp.float32)
    return (
        layer_output,
        input_grad.reshape(seq_count, piece_len, model_width),
        attn_sum[:, : 3 * model_width],
        attn_sum[:, 3 * model_width :],
        ffn_sum[:, 0, :].T,
        ffn_sum[:, 1, :],
        small_sum[0],
        small_sum[1],
        small_sum[2],
        small_sum[3],
        small_sum[4],
        bias_sum,
    )


def solution(mesh):
    placed = (
        P(("fsdp", "tensor"), "ctx", None),
        P(("fsdp", "tensor"), "ctx", None),
        P(("fsdp", "tensor"), "ctx"),
        P(("fsdp", "tensor"), "ctx"),
        P("fsdp", None),
        P("fsdp", None),
        P("fsdp", "tensor"),
        P("tensor", "fsdp"),
        P("fsdp"),
        P("fsdp"),
        P("fsdp"),
        P("fsdp"),
        P("fsdp"),
        P("fsdp"),
    )
    return jax.shard_map(
        shards,
        mesh=mesh,
        in_specs=placed,
        out_specs=(
            P(("fsdp", "tensor"), "ctx", None),
            P(("fsdp", "tensor"), "ctx", None),
            P("fsdp", None),
            P("fsdp", None),
            P("fsdp", "tensor"),
            P("tensor", "fsdp"),
            P("fsdp"),
            P("fsdp"),
            P("fsdp"),
            P("fsdp"),
            P("fsdp"),
            P("fsdp"),
        ),
        check_vma=False,
    )
```

profile of v0, /device:TPU:0, one launch (start us, length us, event | category | flops | bytes accessed | tf_op | source)
XLA Modules:
  0.0 541.3 jit_solution(9679620210667269703)
XLA Ops:
  10.1 1.4 fusion.104
  13.8 11.5 %all-reduce.9 = (bf16[768]{0:T(1024)(128)(2,1)S(1)}, bf16[768]{0:T(1024)(128)(2,1)S(1)}) all-reduce(bf16[768]{0:T(1024)(128)(2,1)S(1)} %dynamic-update-slice.3, bf16[768]{0:T(1024)(128)(2,1)S(1)} %dynamic-update-slice.2), channel_id=1, replica_groups=mesh['fsdp'=4,'ctx'=4,'tensor'=2] {'fsdp'}, use_global_device_ids=true, to_apply=%add.3 | all-reduce | flops 1536 | bytes 6144
  26.0 7.2 %all-gather = bf16[4,1,768]{2,1,0:T(2,128)(2,1)S(1)} all-gather(bf16[1,1,768]{2,1,0:T(2,128)(2,1)S(1)} %reshape.746), channel_id=1, replica_groups=mesh['fsdp'=4,'ctx'=4,'tensor'=2] {'fsdp'}, dimensions={0}, use_global_device_ids=true | all-gather | bytes 7680 | tf_op jit(solution)/shard_map/all_gather | solution.py:121
  35.0 2.4 all_gather.42
  37.4 2.4 all_gather.47
  39.7 10.2 %all-gather.10.cloned.1.call-done = bf16[768,1536]{1,0:T(8,128)(2,1)} async-done(((bf16[192,1536]{1,0:T(8,128)(2,1)}), bf16[768,1536]{1,0:T(8,128)(2,1)}) %all-gather.10.cloned.1.call-update) | async-done | bytes 2359312 | tf_op jit(solution)/shard_map/all_gather | solution.py:114
  50.0 11.0 %multiply_convert_fusion.2 = (bf16[512,1536]{1,0:T(8,128)(2,1)}, f32[512,1536]{1,0:T(8,128)}, f32[512,1536]{1,0:T(8,128)}) fusion(f32[1536]{0:T(1024)S(1)} %dynamic_slice.29, bf16[512,768]{1,0:T(8,128)(2,1)S(1)} %bitcast.296, bf16[768,1536]{1,0:T(8,128)(2,1)} %all-gather.10.cloned.1.call-done), kind=kOutput, calls=%fused_computation.30 | convolution fusion | flops 1259864064 | bytes 11016192 | tf_op jit(solution)/shard_map/dot_general | solution.py:201
  61.0 28.2 %all-gather.12.cloned.1.call-done = bf16[1536,768]{0,1:T(8,128)(2,1)} async-done(((bf16[1536,192]{0,1:T(8,128)(2,1)}), bf16[1536,768]{0,1:T(8,128)(2,1)}) %all-gather.12.cloned.1.call-update) | async-done | bytes 2359312 | tf_op jit(solution)/shard_map/all_gather | solution.py:115
  89.2 5.9 %convert_reduce_fusion = (bf16[1536]{0:T(1024)(128)(2,1)S(1)}, bf16[512,1536]{1,0:T(8,128)(2,1)S(1)}) fusion(f32[512,1536]{1,0:T(8,128)} %get-tuple-element.57, f32[512,1536]{1,0:T(8,128)} %get-tuple-element.91, bf16[512,768]{1,0:T(8,128)(2,1)S(1)} %bitcast.294, bf16[1536,768]{0,1:T(8,128)(2,1)} %all-gather.12.cloned.1.call-done), kind=kOutput, calls=%fused_computation.24 | convolution fusion | flops 1220540928 | bytes 11013120 | tf_op jit(solution)/shard_map/td,fd->tf/dot_general | solution.py:208
  95.1 2.3 convolution_convert_fusion.4
  97.5 3.0 fusion.16
  100.5 1.4 fusion.17
  101.9 2.5 pad_maximum_fusion.1
  104.5 12.7 %copy.65 = bf16[1536,2,768]{0,1,2:T(2,128)(2,1)} copy(bf16[1536,2,768]{2,0,1:T(8,128)(2,1)} %pad_maximum_fusion.1) | data formatting | bytes 9437184 | tf_op jit(solution)/shard_map/stack | solution.py:216
  119.7 4.7 all-to-all-start.1
  125.8 1.9 convolution_convert_fusion.6
  128.8 16.1 %all-reduce.8 = (bf16[768]{0:T(1024)(128)(2,1)S(1)}, bf16[768]{0:T(1024)(128)(2,1)S(1)}, bf16[3072]{0:T(1024)(128)(2,1)}, bf16[768]{0:T(1024)(128)(2,1)}) all-reduce(bf16[768]{0:T(1024)(128)(2,1)S(1)} %dynamic-update-slice.1, bf16[768]{0:T(1024)(128)(2,1)S(1)} %dynamic-update-slice, ...), channel_id=1, replica_groups=mesh['fsdp'=4,'ctx'=4,'tensor'=2] {'fsdp'}, use_global_device_ids=true, to_apply=%add.1 | all-reduce | flops 5376 | bytes 21504
  144.9 22.7 %all-gather.6.cloned.1.call-done = bf16[768,2304]{1,0:T(8,128)(2,1)} async-done(((bf16[192,2304]{1,0:T(8,128)(2,1)}), bf16[768,2304]{1,0:T(8,128)(2,1)}) %all-gather.6.cloned.1.call-update) | async-done | bytes 3538960 | tf_op jit(solution)/shard_map/all_gather | solution.py:112
  167.6 4.5 copy.53
  172.2 2.3 fusion.73
  174.7 4.6 all-to-all-start.3
  180.7 10.1 %all-to-all-done.3 = bf16[1,256,1,12,64]{1,4,2,0,3:T(8,128)(2,1)S(1)} async-done(((bf16[1,256,1,12,64]{1,4,2,0,3:T(8,128)(2,1)}), bf16[1,256,1,12,64]{1,4,2,0,3:T(8,128)(2,1)S(1)}, u32[]{:S(2)}, u32[]{:S(2)}) %all-to-all-start.3) | async-done | bytes 393248 | tf_op jit(solution)/shard_map/all_to_all | solution.py:225
  190.8 3.5 all-to-all-start
  197.9 4.7 convolution_convert_fusion.5
  204.3 18.1 %all-to-all-done = bf16[1,256,3,12,64]{1,4,2,0,3:T(8,128)(2,1)S(1)} async-done(((bf16[1,256,3,12,64]{1,4,2,0,3:T(8,128)(2,1)}), bf16[1,256,3,12,64]{1,4,2,0,3:T(8,128)(2,1)S(1)}, u32[]{:S(2)}, u32[]{:S(2)}) %all-to-all-start) | async-done | bytes 1179680 | tf_op jit(solution)/shard_map/all_to_all | solution.py:148
  222.4 1.9 copy.81
  224.3 2.8 all_to_all.56
  227.2 1.4 fusion.3
  228.6 1.8 fusion.1
  230.5 2.9 fusion.5
  233.3 4.5 multiply_reduce_fusion
  237.9 1.4 fusion.2
  239.3 1.8 fusion
  241.9 4.5 multiply_reduce_fusion.1
  246.3 9.2 %multiply_convert_fusion = (bf16[3,512,1024]{2,1,0:T(8,128)(2,1)S(1)}, bf16[3,512,1024]{2,1,0:T(8,128)(2,1)S(1)}) fusion(f32[3,512,1024]{2,1,0:T(8,128)} %get-tuple-element.99, f32[3,512]{1,0:T(4,128)S(1)} %get-tuple-element.98, f32[3,512]{1,0:T(4,128)S(1)} %log_add_fusion, f32[3,512,1024]{2,1,0:T(8,128)S(1)} %get-tuple-element.93, ...), kind=kLoop, calls=%fused_computation | loop fusion | flops 22020096 | bytes 32530432 | tf_op jit(solution)/shard_map/convert_element_type | solution.py:243
  258.6 2.0 fusion.33
  263.5 4.6 copy.62
  268.2 3.1 reshape.771
  271.3 4.4 all-to-all-start.4
  275.7 5.4 %fusion.41 = bf16[1,512,3,64]{1,3,2,0:T(8,128)(2,1)S(1)} fusion(f32[3,512,1024]{2,1,0:T(8,128)} %copy-done, f32[3,512]{1,0:T(4,128)} %copy-done.31, f32[3,512]{1,0:T(4,128)} %copy-done.30, pred[512,1024]{1,0:T(8,128)(4,1)} %copy-done.9, bf16[1,1024,3,3,64]{1,4,3,2,0:T(8,128)(2,1)} %copy-done.10), kind=kOutput, calls=%fused_computation.84 | convolution fusion | flops 209289216 | bytes 7421952 | tf_op jit(solution)/shard_map/shqk,skhe->sqhe/dot_general | solution.py:183
  281.2 3.0 fusion.40
  285.0 1.4 reshape.769
  286.4 17.8 %all-to-all-done.4 = bf16[4,2,73728]{2,1,0:T(2,128)(2,1)} async-done(((bf16[4,2,73728]{2,1,0:T(2,128)(2,1)}), bf16[4,2,73728]{2,1,0:T(2,128)(2,1)}, u32[]{:S(2)}, u32[]{:S(2)}) %all-to-all-start.4) | async-done | bytes 1179680 | tf_op jit(solution)/shard_map/all_to_all | solution.py:70
  304.2 4.1 all-to-all-start.2
  308.4 3.6 reshape.772
  312.0 3.7 copy.63
  317.0 1.5 slice_bitcast_fusion.1
  320.7 2.9 fusion.62
  324.6 3.1 constant_dynamic-slice_fusion
  327.8 1.6 reshape.770
  333.0 1.3 convolution_convert_fusion
  334.3 2.8 pad_maximum_fusion
  339.3 1.3 dynamic-slice.8
  340.6 2.3 fusion.31
  345.6 1.4 fusion.59
  347.0 2.8 reduce-scatter.13.cloned.1.call-done
  350.6 17.0 %all-reduce.7 = (bf16[5,192]{1,0:T(8,128)(2,1)S(1)}, bf16[768]{0:T(1024)(128)(2,1)S(1)}) all-reduce(bf16[5,192]{1,0:T(8,128)(2,1)S(1)} %copy.70, bf16[768]{0:T(1024)(128)(2,1)} %dynamic-slice.8), channel_id=1, replica_groups=mesh['fsdp'=4,'ctx'=4,'tensor'=2] {'ctx','tensor'}, use_global_device_ids=true, to_apply=%region_24.25 | all-reduce | flops 1728 | bytes 6912 | tf_op jit(solution)/shard_map/psum | solution.py:310
  368.8 40.1 %all-reduce.16.cloned.1.call-done = bf16[1536,2,192]{0,1,2:T(2,128)(2,1)} async-done(((bf16[1536,2,192]{0,1,2:T(2,128)(2,1)}), bf16[1536,2,192]{0,1,2:T(2,128)(2,1)}) %all-reduce.16.cloned.1.call-update) | async-done | bytes 1179664 | tf_op jit(solution)/shard_map/psum | solution.py:313
  408.9 3.7 fusion.102
  412.6 55.6 %reduce-scatter.11.cloned.1.call-done = bf16[192,3072]{1,0:T(8,128)(2,1)} async-done(((bf16[768,3072]{1,0:T(8,128)(2,1)}), bf16[192,3072]{1,0:T(8,128)(2,1)}) %reduce-scatter.11.cloned.1.call-update) | async-done | bytes 1179664 | tf_op jit(solution)/shard_map/reduce_scatter | solution.py:282
  468.2 1.6 copy_bitcast_fusion
  469.7 60.6 %all-reduce.14.cloned.1.call-done = bf16[192,3072]{1,0:T(8,128)(2,1)} async-done(((bf16[192,3072]{1,0:T(8,128)(2,1)}), bf16[192,3072]{1,0:T(8,128)(2,1)}) %all-reduce.14.cloned.1.call-update) | async-done | bytes 1179664 | tf_op jit(solution)/shard_map/psum | solution.py:309
  530.3 1.8 slice.145
  532.1 2.5 slice.144
  (214 shorter events, 39.6 us)
Async XLA Ops:
  7.2 27.3 %copy-start.3 = (bf16[1,256,768]{2,1,0:T(8,128)(2,1)S(1)}, bf16[1,256,768]{2,1,0:T(8,128)(2,1)}, u32[]{:S(2)}) copy-start(bf16[1,256,768]{2,1,0:T(8,128)(2,1)} %param.14) | copy-start | bytes 1179652
  7.2 30.2 %copy-start.5 = (bf16[1,256,768]{2,1,0:T(8,128)(2,1)S(1)}, bf16[1,256,768]{2,1,0:T(8,128)(2,1)}, u32[]{:S(2)}) copy-start(bf16[1,256,768]{2,1,0:T(8,128)(2,1)} %param.15) | copy-start | bytes 1179652
  7.2 42.8 %all-gather.10.cloned.1.call-start = ((), (), s32[]{:S(2)}) async-start(), calls=%async_computation.11 | async-start | bytes 2949120 | tf_op jit(solution)/shard_map/all_gather | solution.py:114
  7.9 81.3 %all-gather.12.cloned.1.call-start = ((), (), s32[]{:S(2)}) async-start(), calls=%async_computation.12 | async-start | bytes 2949120 | tf_op jit(solution)/shard_map/all_gather | solution.py:115
  8.7 117.2 %all-gather.8.cloned.1.call-start = ((), (), s32[]{:S(2)}) async-start(), calls=%async_computation.10 | async-start | bytes 1474560 | tf_op jit(solution)/shard_map/all_gather | solution.py:113
  9.4 158.2 %all-gather.6.cloned.1.call-start = ((), (), s32[]{:S(2)}) async-start(), calls=%async_computation.9 | async-start | bytes 4423680 | tf_op jit(solution)/shard_map/all_gather | solution.py:112
  10.0 192.6 %reduce-scatter.9.cloned.1.call-start = ((), (), s32[]{:S(2)}) async-start(), calls=%async_computation.14 | async-start | bytes 1179648 | tf_op jit(solution)/shard_map/reduce_scatter | solution.py:74
  26.0 9.0 %copy-start.24 = (f32[768]{0:T(1024)}, f32[768]{0:T(1024)S(1)}, u32[]{:S(2)}) copy-start(f32[768]{0:T(1024)S(1)} %convert_element_type.220) | copy-start | bytes 9220
  34.4 2.9 copy-start.21
  34.7 2.7 copy-start.27
  89.2 5.9 %copy-start.39 = (bf16[768,1536]{1,0:T(8,128)(2,1)S(1)}, bf16[768,1536]{1,0:T(8,128)(2,1)}, u32[]{:S(2)}) copy-start(bf16[768,1536]{1,0:T(8,128)(2,1)} %all-gather.10.cloned.1.call-done) | copy-start | bytes 7077892
  95.1 2.3 copy-start.45
  97.4 227.2 %all-reduce.18.cloned.1.call-start = ((), (), s32[]{:S(2)}) async-start(), calls=%async_computation.19 | async-start | bytes 9437184
  97.5 3.0 copy-start.44
  117.2 7.2 %copy-start.38 = (s32[1,256]{1,0:T(1,128)S(1)}, s32[1,256]{1,0:T(1,128)}, u32[]{:S(2)}) copy-start(s32[1,256]{1,0:T(1,128)} %param.17) | copy-start | bytes 3076
  117.2 7.2 %copy-start.41 = (bf16[192]{0:T(256)(128)(2,1)S(1)}, bf16[192]{0:T(256)(128)(2,1)}, u32[]{:S(2)}) copy-start(bf16[192]{0:T(256)(128)(2,1)} %param.22) | copy-start | bytes 1156
  117.2 7.5 %copy-start.42 = (bf16[192]{0:T(256)(128)(2,1)S(1)}, bf16[192]{0:T(256)(128)(2,1)}, u32[]{:S(2)}) copy-start(bf16[192]{0:T(256)(128)(2,1)} %param.23) | copy-start | bytes 1156
  117.2 7.7 %copy-start.43 = (bf16[192]{0:T(256)(128)(2,1)S(1)}, bf16[192]{0:T(256)(128)(2,1)}, u32[]{:S(2)}) copy-start(bf16[192]{0:T(256)(128)(2,1)} %param.26) | copy-start | bytes 1156
  119.7 55.0 %all-to-all-start.1 = ((bf16[4,2,128]{2,1,0:T(2,128)(2,1)}), bf16[4,2,128]{2,1,0:T(2,128)(2,1)}, u32[]{:S(2)}, u32[]{:S(2)}) async-start(bf16[4,2,128]{2,1,0:T(2,128)(2,1)} %reshape.767), calls=%async_computation.1 | async-start | bytes 4096 | tf_op jit(solution)/shard_map/all_to_all | solution.py:149
  174.4 4.8 copy-start.19
  174.7 16.1 %all-to-all-start.3 = ((bf16[1,256,1,12,64]{1,4,2,0,3:T(8,128)(2,1)}), bf16[1,256,1,12,64]{1,4,2,0,3:T(8,128)(2,1)S(1)}, u32[]{:S(2)}, u32[]{:S(2)}) async-start(bf16[1,256,1,12,64]{1,4,2,0,3:T(8,128)(2,1)} %bitcast.40), calls=%async_computation.4 | async-start | bytes 786432 | tf_op jit(solution)/shard_map/all_to_all | solution.py:225
  179.4 15.0 %copy-start.6 = (bf16[1,256,768]{2,1,0:T(8,128)(2,1)S(1)}, bf16[1,256,768]{2,1,0:T(8,128)(2,1)}, u32[]{:S(2)}) copy-start(bf16[1,256,768]{2,1,0:T(8,128)(2,1)} %param.15) | copy-start | bytes 1179652
  190.8 31.6 %all-to-all-start = ((bf16[1,256,3,12,64]{1,4,2,0,3:T(8,128)(2,1)}), bf16[1,256,3,12,64]{1,4,2,0,3:T(8,128)(2,1)S(1)}, u32[]{:S(2)}, u32[]{:S(2)}) async-start(bf16[1,256,3,12,64]{1,4,2,0,3:T(8,128)(2,1)} %copy.54), calls=%async_computation | async-start | bytes 2359296 | tf_op jit(solution)/shard_map/all_to_all | solution.py:148
  194.3 146.2 %reduce-scatter.7.cloned.1.call-start = ((), (), s32[]{:S(2)}) async-start(), calls=%async_computation.13 | async-start | bytes 1179648 | tf_op jit(solution)/shard_map/reduce_scatter | solution.py:74
  197.3 49.1 %copy-start.9 = (pred[512,1024]{1,0:T(8,128)(4,1)}, pred[512,1024]{1,0:T(8,128)(4,1)S(1)}, u32[]{:S(2)}) copy-start(pred[512,1024]{1,0:T(8,128)(4,1)S(1)} %get-tuple-element.86) | copy-start | bytes 1572868
  197.3 60.0 %copy-start.7 = (pred[512,1024]{1,0:T(8,128)(4,1)}, pred[512,1024]{1,0:T(8,128)(4,1)S(1)}, u32[]{:S(2)}) copy-start(pred[512,1024]{1,0:T(8,128)(4,1)S(1)} %get-tuple-element.85) | copy-start | bytes 1572868
  197.9 43.2 %copy-start.17 = (bf16[1,1024,3,64]{1,3,2,0:T(8,128)(2,1)}, bf16[1,1024,3,64]{1,3,2,0:T(8,128)(2,1)S(1)}, u32[]{:S(2)}) copy-start(bf16[1,1024,3,64]{1,3,2,0:T(8,128)(2,1)S(1)} %squeeze.45) | copy-start | bytes 1179652
  227.1 33.4 %copy-start.10 = (bf16[1,1024,3,3,64]{1,4,3,2,0:T(8,128)(2,1)}, bf16[1,1024,3,3,64]{1,4,3,2,0:T(8,128)(2,1)S(1)}, u32[]{:S(2)}) copy-start(bf16[1,1024,3,3,64]{1,4,3,2,0:T(8,128)(2,1)S(1)} %all_to_all.56) | copy-start | bytes 3538948
  228.6 1.9 copy-start.30
  228.6 17.8 %copy-start = (f32[3,512,1024]{2,1,0:T(8,128)}, f32[3,512,1024]{2,1,0:T(8,128)S(1)}, u32[]{:S(2)}) copy-start(f32[3,512,1024]{2,1,0:T(8,128)S(1)} %get-tuple-element.93) | copy-start | bytes 18874372
  230.4 2.9 copy-start.31
  239.2 1.8 copy-start.32
  239.2 2.6 copy-start.1
  241.0 5.3 copy-start.34
  255.5 2.8 copy-start.2
  255.5 2.8 copy-start.18
  255.5 3.0 copy-start.46
  271.3 9.9 %slice-start = ((s8[6291456]{0:T(1024)(128)(4,1)}), s8[2097152]{0:T(1024)(128)(4,1)S(1)}, s32[]{:S(2)}) async-start(s8[6291456]{0:T(1024)(128)(4,1)} %bitcast.274), calls=%async_computation.20 | async-start | bytes 4194304
  271.3 32.9 %all-to-all-start.4 = ((bf16[4,2,73728]{2,1,0:T(2,128)(2,1)}), bf16[4,2,73728]{2,1,0:T(2,128)(2,1)}, u32[]{:S(2)}, u32[]{:S(2)}) async-start(bf16[4,2,73728]{2,1,0:T(2,128)(2,1)} %reshape.771), calls=%async_computation.5 | async-start | bytes 2359296 | tf_op jit(solution)/shard_map/all_to_all | solution.py:70
  275.7 5.5 %slice-start.1 = ((s8[6291456]{0:T(1024)(128)(4,1)}), s8[4194304]{0:T(1024)(128)(4,1)S(1)}, s32[]{:S(2)}) async-start(s8[6291456]{0:T(1024)(128)(4,1)} %bitcast.274), calls=%async_computation.21 | async-start | bytes 8388608
  275.7 5.5 %copy-start.8 = (pred[512,1024]{1,0:T(8,128)(4,1)S(1)}, pred[512,1024]{1,0:T(8,128)(4,1)}, u32[]{:S(2)}) copy-start(pred[512,1024]{1,0:T(8,128)(4,1)} %copy-done.7) | copy-start | bytes 1572868
  275.7 5.5 %copy-start.33 = (f32[3,512]{1,0:T(4,128)S(1)}, f32[3,512]{1,0:T(4,128)}, u32[]{:S(2)}) copy-start(f32[3,512]{1,0:T(4,128)} %copy-done.32) | copy-start | bytes 18436
  275.7 5.5 %copy-start.35 = (f32[3,512]{1,0:T(4,128)S(1)}, f32[3,512]{1,0:T(4,128)}, u32[]{:S(2)}) copy-start(f32[3,512]{1,0:T(4,128)} %copy-done.34) | copy-start | bytes 18436
  304.2 23.6 %all-to-all-start.2 = ((bf16[4,2,24576]{2,1,0:T(2,128)(2,1)}), bf16[4,2,24576]{2,1,0:T(2,128)(2,1)}, u32[]{:S(2)}, u32[]{:S(2)}) async-start(bf16[4,2,24576]{2,1,0:T(2,128)(2,1)} %reshape.769), calls=%async_computation.2 | async-start | bytes 786432 | tf_op jit(solution)/shard_map/all_to_all | solution.py:70
  308.3 41.4 %reduce-scatter.13.cloned.1.call-start = ((), (), s32[]{:S(2)}) async-start(), calls=%async_computation.18 | async-start | bytes 245760
  315.8 2.9 copy-start.20
  318.5 1.0 copy-start.4
  318.5 2.1 copy-start.11
  318.5 2.2 copy-start.12
  318.5 2.2 copy-start.22
  318.5 2.1 copy-start.25
  318.5 2.1 copy-start.28
  320.7 2.9 copy-start.36
  320.7 2.9 copy-start.37
  324.5 84.3 %all-reduce.16.cloned.1.call-start = ((), (), s32[]{:S(2)}) async-start(), calls=%async_computation.17 | async-start | bytes 2359296 | tf_op jit(solution)/shard_map/psum | solution.py:313
  327.7 5.3 copy-start.23
  327.7 5.3 copy-start.29
  327.7 140.4 %reduce-scatter.11.cloned.1.call-start = ((), (), s32[]{:S(2)}) async-start(), calls=%async_computation.15 | async-start | bytes 5898240 | tf_op jit(solution)/shard_map/reduce_scatter | solution.py:282
  331.7 0.7 copy-start.13
  337.1 3.5 copy-start.14
  337.1 3.5 copy-start.15
  337.1 8.5 %copy-start.16 = (f32[256,768]{1,0:T(8,128)S(1)}, f32[256,768]{1,0:T(8,128)}, u32[]{:S(2)}) copy-start(f32[256,768]{1,0:T(8,128)} %get-tuple-element.100) | copy-start | bytes 2359300
  337.1 8.5 %copy-start.26 = (f32[768]{0:T(1024)S(1)}, f32[768]{0:T(1024)}, u32[]{:S(2)}) copy-start(f32[768]{0:T(1024)} %copy-done.24) | copy-start | bytes 9220
  337.1 193.2 %all-reduce.14.cloned.1.call-start = ((), (), s32[]{:S(2)}) async-start(), calls=%async_computation.16 | async-start | bytes 2359296 | tf_op jit(solution)/shard_map/psum | solution.py:309
  (1 other events, 0.7 us)
Sparse Core Ops, SparseCore 0:
  9.8 40.0 all-gather.9
  51.8 37.3 all-gather.11
  91.0 27.5 all-gather.7
  120.4 47.2 all-gather.5
  170.3 8.1 reduce-scatter.8
  181.6 113.3 all-reduce.17
  297.9 8.1 reduce-scatter.6
  324.6 25.0 reduce-scatter.12
  352.7 56.1 all-reduce.15
  411.7 56.3 reduce-scatter.10
  470.5 59.7 all-reduce.13
where the time goes:
time: 552 us; the launch traced here: 541 us
  waiting for transfers between devices  269 us (49%)
  local copies, waits for them, and re-layouts  78.2 us (14%)
  matrix products  67.9 us (12%)
  blocking collectives  56.5 us (10%)
  other arithmetic  30.6 us (6%)
  starting transfers between devices  21.8 us (4%)
  between operations  17.2 us (3%)
    psum x1, waiting for transfers between devices, shards(): lax.psum(attn_grad, ('ctx', 'tensor')).astype(jnp.float32)  60.6 us
    reduce_scatter x1, waiting for transfers between devices, shards(): lax.psum_scatter(jnp.concatenate([qkv_part, proj_part], axis=1).astype(jn...  55.6 us
    psum x1, waiting for transfers between devices, shards(): ffn_sum = lax.psum(ffn_part.astype(jnp.bfloat16), 'ctx').astype(jnp.float32)  40.1 us
    unnamed x126, local copies, waits for them, and re-layouts  29.1 us
    all_gather x1, waiting for transfers between devices, shards(): lax.all_gather(down_matrix, 'fsdp', axis=1, tiled=True)  28.2 us
    unnamed x2, blocking collectives  27.5 us
    all_gather x1, waiting for transfers between devices, shards(): lax.all_gather(query_key_value_weight, 'fsdp', axis=0, tiled=True)  22.7 us
    all_to_all x1, waiting for transfers between devices, shards(): lax.all_to_all(packed, 'ctx', split_axis=3, concat_axis=1, tiled=True)  18.1 us
  transfers between devices with their start and end apart: 16, of which 10 were waited for; matrix products, arithmetic and copies ran while one was open for 30% of the time, Pallas kernels for 0%

commit v1 on v0

--- a/solution.py
+++ b/solution.py
@@ -310,7 +310,9 @@
         lax.psum(small_part.astype(jnp.bfloat16), ("ctx", "tensor")).astype(jnp.float32),
         lax.psum(bias_part.astype(jnp.bfloat16), ("ctx", "tensor")).astype(jnp.float32),
     )
-    ffn_sum = lax.psum(ffn_part.astype(jnp.bfloat16), "ctx").astype(jnp.float32)
+    ffn_sum = jnp.sum(lax.all_gather(ffn_part.astype(jnp.bfloat16), "ctx"), axis=0).astype(
+        jnp.float32
+    )
     return (
         layer_output,
         input_grad.reshape(seq_count, piece_len, model_width),

time: 552 us -> 609 us (1.10)
  waiting for transfers between devices: 269 us -> 290 us
  blocking collectives: 56.5 us -> 70.9 us
  local copies, waits for them, and re-layouts: 78.2 us -> 89.3 us
  other arithmetic: 30.6 us -> 39.6 us
    all_gather x0 -> x1, waiting for transfers between devices: none -> 62.3 us  [shards(): lax.all_gather(ffn_part.astype(jnp.bfloat16), 'ctx')]
    psum x1 -> x0, waiting for transfers between devices: 40.1 us -> none  [shards(): ffn_sum = lax.psum(ffn_part.astype(jnp.bfloat16), 'ctx').astype(jnp.float32)]
    all_to_all x1, waiting for transfers between devices: 18.1 us -> 0.5 us  [shards(): lax.all_to_all(packed, 'ctx', split_axis=3, concat_axis=1, tiled=True)]
    reduce_scatter x1, waiting for transfers between devices: 55.6 us -> 38.8 us  [shards(): lax.psum_scatter(jnp.concatenate([qkv_part, proj_part], axis=1).astype(jn...]
    all_to_all x0 -> x1, blocking collectives: none -> 16.5 us  [to_tokens(): lax.all_to_all(blocks, 'ctx', split_axis=1, concat_axis=3, tiled=True)]
    unnamed x13, waiting for transfers between devices: 5.47 us -> 21.9 us
    all_gather x1, waiting for transfers between devices: 10.2 us -> 25.7 us  [shards(): lax.all_gather(up_matrix, 'fsdp', axis=0, tiled=True)]
    all_gather x0 -> x1, local copies, waits for them, and re-layouts: none -> 12 us  [shards(): lax.all_gather(ffn_part.astype(jnp.bfloat16), 'ctx')]
  transfers between devices with their start and end apart: 16 -> 15, of which waited for: 10 -> 10; matrix products, arithmetic and copies ran while one was open for 30% -> 32% of each run, Pallas kernels for 0% -> 0%
where the time goes in v1:
time: 609 us; the launch traced here: 598 us
  waiting for transfers between devices  290 us (48%)
  local copies, waits for them, and re-layouts  89.3 us (15%)
  matrix products  71.6 us (12%)
  blocking collectives  70.9 us (12%)
  other arithmetic  39.6 us (7%)
  starting transfers between devices  19.9 us (3%)
  between operations  17.2 us (3%)
    all_gather x1, waiting for transfers between devices, shards(): lax.all_gather(ffn_part.astype(jnp.bfloat16), 'ctx')  62.3 us
    psum x1, waiting for transfers between devices, shards(): lax.psum(attn_grad, ('ctx', 'tensor')).astype(jnp.float32)  55.9 us
    reduce_scatter x1, waiting for transfers between devices, shards(): lax.psum_scatter(jnp.concatenate([qkv_part, proj_part], axis=1).astype(jn...  38.8 us
    unnamed x127, local copies, waits for them, and re-layouts  31.9 us
    all_gather x1, waiting for transfers between devices, shards(): lax.all_gather(down_matrix, 'fsdp', axis=1, tiled=True)  28.3 us
    unnamed x2, blocking collectives  26.2 us
    all_gather x1, waiting for transfers between devices, shards(): lax.all_gather(up_matrix, 'fsdp', axis=0, tiled=True)  25.7 us
    all_gather x1, waiting for transfers between devices, shards(): lax.all_gather(query_key_value_weight, 'fsdp', axis=0, tiled=True)  25.6 us
  transfers between devices with their start and end apart: 15, of which 10 were waited for; matrix products, arithmetic and copies ran while one was open for 32% of the time, Pallas kernels for 0%

profile of v1, /device:TPU:0, one launch (start us, length us, event | category | flops | bytes accessed | tf_op | source)
XLA Modules:
  0.0 598.0 jit_solution(12744581481940037379)
XLA Ops:
  12.5 6.3 %all-to-all-start.1 = ((bf16[4,2,128]{2,1,0:T(2,128)(2,1)}), bf16[4,2,128]{2,1,0:T(2,128)(2,1)}, u32[]{:S(2)}, u32[]{:S(2)}) async-start(bf16[4,2,128]{2,1,0:T(2,128)(2,1)} %reshape.768), calls=%async_computation.1 | async-start | bytes 4096 | tf_op jit(solution)/shard_map/all_to_all | solution.py:149
  19.5 1.3 fusion.103
  23.2 9.9 %all-reduce.9 = (bf16[768]{0:T(1024)(128)(2,1)S(1)}, bf16[768]{0:T(1024)(128)(2,1)S(1)}) all-reduce(bf16[768]{0:T(1024)(128)(2,1)S(1)} %dynamic-update-slice.2, bf16[768]{0:T(1024)(128)(2,1)S(1)} %dynamic-update-slice.3), channel_id=1, replica_groups=mesh['fsdp'=4,'ctx'=4,'tensor'=2] {'fsdp'}, use_global_device_ids=true, to_apply=%add.2 | all-reduce | flops 1536 | bytes 6144
  33.8 7.4 %all-gather.1 = bf16[4,1,768]{2,1,0:T(2,128)(2,1)S(1)} all-gather(bf16[1,1,768]{2,1,0:T(2,128)(2,1)S(1)} %reshape.747), channel_id=1, replica_groups=mesh['fsdp'=4,'ctx'=4,'tensor'=2] {'fsdp'}, dimensions={0}, use_global_device_ids=true | all-gather | bytes 7680 | tf_op jit(solution)/shard_map/all_gather | solution.py:121
  45.5 2.4 all_gather.48
  47.9 2.4 all_gather.53
  51.1 1.8 convolution_convert_fusion.6
  53.8 25.7 %all-gather.12.cloned.1.call-done = bf16[768,1536]{1,0:T(8,128)(2,1)} async-done(((bf16[192,1536]{1,0:T(8,128)(2,1)}), bf16[768,1536]{1,0:T(8,128)(2,1)}) %all-gather.12.cloned.1.call-update) | async-done | bytes 2359312 | tf_op jit(solution)/shard_map/all_gather | solution.py:114
  79.5 11.0 %multiply_convert_fusion.2 = (bf16[512,1536]{1,0:T(8,128)(2,1)}, f32[512,1536]{1,0:T(8,128)}, f32[512,1536]{1,0:T(8,128)}) fusion(f32[1536]{0:T(1024)S(1)} %dynamic_slice.29, bf16[512,768]{1,0:T(8,128)(2,1)S(1)} %bitcast.298, bf16[768,1536]{1,0:T(8,128)(2,1)} %all-gather.12.cloned.1.call-done), kind=kOutput, calls=%fused_computation.30 | convolution fusion | flops 1259864064 | bytes 11016192 | tf_op jit(solution)/shard_map/dot_general | solution.py:201
  90.4 28.3 %all-gather.14.cloned.1.call-done = bf16[1536,768]{0,1:T(8,128)(2,1)} async-done(((bf16[1536,192]{0,1:T(8,128)(2,1)}), bf16[1536,768]{0,1:T(8,128)(2,1)}) %all-gather.14.cloned.1.call-update) | async-done | bytes 2359312 | tf_op jit(solution)/shard_map/all_gather | solution.py:115
  118.7 6.9 %convert_reduce_fusion = (bf16[1536]{0:T(1024)(128)(2,1)S(1)}, bf16[512,1536]{1,0:T(8,128)(2,1)}) fusion(f32[512,1536]{1,0:T(8,128)} %get-tuple-element.57, f32[512,1536]{1,0:T(8,128)} %get-tuple-element.91, bf16[512,768]{1,0:T(8,128)(2,1)S(1)} %bitcast.296, bf16[1536,768]{0,1:T(8,128)(2,1)} %all-gather.14.cloned.1.call-done), kind=kOutput, calls=%fused_computation.24 | convolution fusion | flops 1220540928 | bytes 11013120 | tf_op jit(solution)/shard_map/td,fd->tf/dot_general | solution.py:208
  125.8 16.3 %all-reduce.8 = (bf16[768]{0:T(1024)(128)(2,1)S(1)}, bf16[768]{0:T(1024)(128)(2,1)S(1)}, bf16[3072]{0:T(1024)(128)(2,1)}, bf16[768]{0:T(1024)(128)(2,1)}) all-reduce(bf16[768]{0:T(1024)(128)(2,1)S(1)} %dynamic-update-slice.1, bf16[768]{0:T(1024)(128)(2,1)S(1)} %dynamic-update-slice, ...), channel_id=1, replica_groups=mesh['fsdp'=4,'ctx'=4,'tensor'=2] {'fsdp'}, use_global_device_ids=true, to_apply=%add.1 | all-reduce | flops 5376 | bytes 21504
  142.1 25.6 %all-gather.8.cloned.1.call-done = bf16[768,2304]{1,0:T(8,128)(2,1)} async-done(((bf16[192,2304]{1,0:T(8,128)(2,1)}), bf16[768,2304]{1,0:T(8,128)(2,1)}) %all-gather.8.cloned.1.call-update) | async-done | bytes 3538960 | tf_op jit(solution)/shard_map/all_gather | solution.py:112
  167.7 4.5 copy.52
  172.3 2.3 fusion.73
  174.8 4.6 all-to-all-start.3
  180.7 10.1 %all-to-all-done.3 = bf16[1,256,1,12,64]{1,4,2,0,3:T(8,128)(2,1)S(1)} async-done(((bf16[1,256,1,12,64]{1,4,2,0,3:T(8,128)(2,1)}), bf16[1,256,1,12,64]{1,4,2,0,3:T(8,128)(2,1)S(1)}, u32[]{:S(2)}, u32[]{:S(2)}) %all-to-all-start.3) | async-done | bytes 393248 | tf_op jit(solution)/shard_map/all_to_all | solution.py:225
  190.9 3.5 all-to-all-start
  194.8 4.5 convolution_convert_fusion.4
  202.2 3.2 fusion.16
  205.4 1.4 fusion.17
  206.8 2.5 pad_maximum_fusion.1
  209.4 12.6 %copy.64 = bf16[1536,2,768]{0,1,2:T(2,128)(2,1)} copy(bf16[1536,2,768]{2,0,1:T(8,128)(2,1)} %pad_maximum_fusion.1) | data formatting | bytes 9437184 | tf_op jit(solution)/shard_map/stack | solution.py:216
  224.3 1.4 fusion.3
  225.7 1.8 fusion.1
  227.6 1.4 fusion.2
  229.0 1.8 fusion
  230.8 4.6 multiply_reduce_fusion
  235.4 4.5 multiply_reduce_fusion.1
  239.9 9.2 %multiply_convert_fusion = (bf16[3,512,1024]{2,1,0:T(8,128)(2,1)S(1)}, bf16[3,512,1024]{2,1,0:T(8,128)(2,1)S(1)}) fusion(f32[3,512,1024]{2,1,0:T(8,128)} %get-tuple-element.99, f32[3,512]{1,0:T(4,128)S(1)} %get-tuple-element.98, f32[3,512]{1,0:T(4,128)S(1)} %log_add_fusion, f32[3,512,1024]{2,1,0:T(8,128)S(1)} %get-tuple-element.93, ...), kind=kLoop, calls=%fused_computation | loop fusion | flops 22020096 | bytes 32530432 | tf_op jit(solution)/shard_map/convert_element_type | solution.py:243
  252.8 2.0 fusion.5
  255.2 1.9 fusion.33
  258.3 4.7 copy.61
  263.0 3.1 reshape.772
  266.1 4.5 all-to-all-start.4
  270.5 4.5 convolution_convert_fusion.5
  278.1 20.3 %all-to-all-done.4 = bf16[4,2,73728]{2,1,0:T(2,128)(2,1)} async-done(((bf16[4,2,73728]{2,1,0:T(2,128)(2,1)}), bf16[4,2,73728]{2,1,0:T(2,128)(2,1)}, u32[]{:S(2)}, u32[]{:S(2)}) %all-to-all-start.4) | async-done | bytes 1179680 | tf_op jit(solution)/shard_map/all_to_all | solution.py:70
  298.4 3.5 reshape.773
  301.9 3.8 copy.62
  307.0 1.7 slice_bitcast_fusion.3
  311.4 2.9 fusion.62
  315.6 19.2 %all-reduce.15.cloned.1.call-done = bf16[1536,2,768]{0,1,2:T(2,128)(2,1)} async-done(((bf16[1536,2,768]{0,1,2:T(2,128)(2,1)}), bf16[1536,2,768]{0,1,2:T(2,128)(2,1)}) %all-reduce.15.cloned.1.call-update) | async-done | bytes 4718608
  334.8 3.1 constant_dynamic-slice_fusion
  338.1 4.8 fusion.41
  343.0 4.9 fusion.40
  348.6 1.4 reshape.770
  350.1 16.5 %all_to_all.72 = bf16[4,2,24576]{2,1,0:T(2,128)(2,1)} all-to-all(bf16[4,2,24576]{2,1,0:T(2,128)(2,1)} %reshape.770), channel_id=1, replica_groups=mesh['fsdp'=4,'ctx'=4,'tensor'=2] {'ctx'}, dimensions={0} | all-to-all | bytes 786432 | tf_op jit(solution)/shard_map/all_to_all | solution.py:70
  366.5 1.6 reshape.771
  373.0 2.9 pad_maximum_fusion
  378.0 1.3 dynamic-slice.8
  379.3 2.3 fusion.31
  384.3 1.4 fusion.59
  386.6 16.1 %all-reduce.7 = (bf16[5,192]{1,0:T(8,128)(2,1)S(1)}, bf16[768]{0:T(1024)(128)(2,1)S(1)}) all-reduce(bf16[5,192]{1,0:T(8,128)(2,1)S(1)} %copy.73, bf16[768]{0:T(1024)(128)(2,1)} %dynamic-slice.8), channel_id=1, replica_groups=mesh['fsdp'=4,'ctx'=4,'tensor'=2] {'ctx','tensor'}, use_global_device_ids=true, to_apply=%region_24.25 | all-reduce | flops 1728 | bytes 6912 | tf_op jit(solution)/shard_map/psum | solution.py:310
  403.9 62.3 %all-gather.16.cloned.1.call-done = bf16[6144,2,192]{0,1,2:T(2,128)(2,1)} async-done(((bf16[1536,2,192]{0,1,2:T(2,128)(2,1)}), bf16[6144,2,192]{0,1,2:T(2,128)(2,1)}) %all-gather.16.cloned.1.call-update) | async-done | bytes 4718608 | tf_op jit(solution)/shard_map/all_gather | solution.py:313
  466.2 12.0 %copy.71 = bf16[6144,2,192]{2,0,1:T(8,128)(2,1)} copy(bf16[6144,2,192]{0,1,2:T(2,128)(2,1)} %all-gather.16.cloned.1.call-done) | data formatting | bytes 9437184 | tf_op jit(solution)/shard_map/all_gather | solution.py:313
  478.3 5.6 reduce_sum.166
  483.8 1.8 convert_element_type.248
  485.6 38.8 %reduce-scatter.11.cloned.1.call-done = bf16[192,3072]{1,0:T(8,128)(2,1)} async-done(((bf16[768,3072]{1,0:T(8,128)(2,1)}), bf16[192,3072]{1,0:T(8,128)(2,1)}) %reduce-scatter.11.cloned.1.call-update) | async-done | bytes 1179664 | tf_op jit(solution)/shard_map/reduce_scatter | solution.py:282
  524.5 1.9 slice_bitcast_fusion
  526.4 3.0 copy.67
  529.4 1.5 copy.66
  530.9 55.9 %all-reduce.13.cloned.1.call-done = bf16[192,3072]{1,0:T(8,128)(2,1)} async-done(((bf16[192,3072]{1,0:T(8,128)(2,1)}), bf16[192,3072]{1,0:T(8,128)(2,1)}) %all-reduce.13.cloned.1.call-update) | async-done | bytes 1179664 | tf_op jit(solution)/shard_map/psum | solution.py:309
  586.8 1.8 slice.145
  588.6 2.5 slice.144
  (217 shorter events, 46.1 us)
Async XLA Ops:
  7.2 37.8 %copy-start.2 = (bf16[1,256,768]{2,1,0:T(8,128)(2,1)S(1)}, bf16[1,256,768]{2,1,0:T(8,128)(2,1)}, u32[]{:S(2)}) copy-start(bf16[1,256,768]{2,1,0:T(8,128)(2,1)} %param.14) | copy-start | bytes 1179652
  7.2 40.7 %copy-start.4 = (bf16[1,256,768]{2,1,0:T(8,128)(2,1)S(1)}, bf16[1,256,768]{2,1,0:T(8,128)(2,1)}, u32[]{:S(2)}) copy-start(bf16[1,256,768]{2,1,0:T(8,128)(2,1)} %param.15) | copy-start | bytes 1179652
  7.2 43.9 %all-gather.10.cloned.1.call-start = ((), (), s32[]{:S(2)}) async-start(), calls=%async_computation.10 | async-start | bytes 1474560 | tf_op jit(solution)/shard_map/all_gather | solution.py:113
  7.9 71.5 %all-gather.12.cloned.1.call-start = ((), (), s32[]{:S(2)}) async-start(), calls=%async_computation.11 | async-start | bytes 2949120 | tf_op jit(solution)/shard_map/all_gather | solution.py:114
  8.7 110.0 %all-gather.14.cloned.1.call-start = ((), (), s32[]{:S(2)}) async-start(), calls=%async_computation.12 | async-start | bytes 2949120 | tf_op jit(solution)/shard_map/all_gather | solution.py:115
  9.4 158.3 %all-gather.8.cloned.1.call-start = ((), (), s32[]{:S(2)}) async-start(), calls=%async_computation.9 | async-start | bytes 4423680 | tf_op jit(solution)/shard_map/all_gather | solution.py:112
  12.5 162.3 %all-to-all-start.1 = ((bf16[4,2,128]{2,1,0:T(2,128)(2,1)}), bf16[4,2,128]{2,1,0:T(2,128)(2,1)}, u32[]{:S(2)}, u32[]{:S(2)}) async-start(bf16[4,2,128]{2,1,0:T(2,128)(2,1)} %reshape.768), calls=%async_computation.1 | async-start | bytes 4096 | tf_op jit(solution)/shard_map/all_to_all | solution.py:149
  33.1 12.4 %copy-start.30 = (f32[768]{0:T(1024)}, f32[768]{0:T(1024)S(1)}, u32[]{:S(2)}) copy-start(f32[768]{0:T(1024)S(1)} %convert_element_type.222) | copy-start | bytes 9220
  45.0 5.3 copy-start.27
  45.2 5.0 copy-start.33
  47.9 42.6 %copy-start.22 = (bf16[2,256,768]{2,1,0:T(8,128)(2,1)}, bf16[2,256,768]{2,1,0:T(8,128)(2,1)S(1)}, u32[]{:S(2)}) copy-start(bf16[2,256,768]{2,1,0:T(8,128)(2,1)S(1)} %all_gather.48) | copy-start | bytes 2359300
  50.2 68.5 %copy-start.20 = (bf16[2,256,768]{2,1,0:T(8,128)(2,1)}, bf16[2,256,768]{2,1,0:T(8,128)(2,1)S(1)}, u32[]{:S(2)}) copy-start(bf16[2,256,768]{2,1,0:T(8,128)(2,1)S(1)} %all_gather.53) | copy-start | bytes 2359300
  174.5 4.8 copy-start.25
  174.8 16.1 %all-to-all-start.3 = ((bf16[1,256,1,12,64]{1,4,2,0,3:T(8,128)(2,1)}), bf16[1,256,1,12,64]{1,4,2,0,3:T(8,128)(2,1)S(1)}, u32[]{:S(2)}, u32[]{:S(2)}) async-start(bf16[1,256,1,12,64]{1,4,2,0,3:T(8,128)(2,1)} %bitcast.40), calls=%async_computation.4 | async-start | bytes 786432 | tf_op jit(solution)/shard_map/all_to_all | solution.py:225
  190.9 31.6 %all-to-all-start = ((bf16[1,256,3,12,64]{1,4,2,0,3:T(8,128)(2,1)}), bf16[1,256,3,12,64]{1,4,2,0,3:T(8,128)(2,1)S(1)}, u32[]{:S(2)}, u32[]{:S(2)}) async-start(bf16[1,256,3,12,64]{1,4,2,0,3:T(8,128)(2,1)} %copy.53), calls=%async_computation | async-start | bytes 2359296 | tf_op jit(solution)/shard_map/all_to_all | solution.py:148
  194.4 82.0 %reduce-scatter.9.cloned.1.call-start = ((), (), s32[]{:S(2)}) async-start(), calls=%async_computation.14 | async-start | bytes 1179648 | tf_op jit(solution)/shard_map/reduce_scatter | solution.py:74
  199.3 135.5 %all-reduce.15.cloned.1.call-start = ((), (), s32[]{:S(2)}) async-start(), calls=%async_computation.19 | async-start | bytes 9437184
  200.8 51.9 %copy-start.9 = (pred[512,1024]{1,0:T(8,128)(4,1)}, pred[512,1024]{1,0:T(8,128)(4,1)S(1)}, u32[]{:S(2)}) copy-start(pred[512,1024]{1,0:T(8,128)(4,1)S(1)} %get-tuple-element.86) | copy-start | bytes 1572868
  200.9 53.9 %copy-start.7 = (pred[512,1024]{1,0:T(8,128)(4,1)}, pred[512,1024]{1,0:T(8,128)(4,1)S(1)}, u32[]{:S(2)}) copy-start(pred[512,1024]{1,0:T(8,128)(4,1)S(1)} %get-tuple-element.85) | copy-start | bytes 1572868
  202.2 3.2 copy-start.21
  202.2 3.2 copy-start.46
  224.3 26.0 %copy-start.11 = (bf16[1,1024,3,3,64]{1,4,3,2,0:T(8,128)(2,1)}, bf16[1,1024,3,3,64]{1,4,3,2,0:T(8,128)(2,1)S(1)}, u32[]{:S(2)}) copy-start(bf16[1,1024,3,3,64]{1,4,3,2,0:T(8,128)(2,1)S(1)} %all_to_all.56) | copy-start | bytes 3538948
  225.7 1.9 copy-start.36
  225.7 27.0 %copy-start = (f32[3,512,1024]{2,1,0:T(8,128)}, f32[3,512,1024]{2,1,0:T(8,128)S(1)}, u32[]{:S(2)}) copy-start(f32[3,512,1024]{2,1,0:T(8,128)S(1)} %get-tuple-element.93) | copy-start | bytes 18874372
  227.6 1.4 copy-start.38
  229.0 1.8 copy-start.40
  229.0 6.4 %copy-start.1 = (f32[3,512,1024]{2,1,0:T(8,128)}, f32[3,512,1024]{2,1,0:T(8,128)S(1)}, u32[]{:S(2)}) copy-start(f32[3,512,1024]{2,1,0:T(8,128)S(1)} %get-tuple-element.95) | copy-start | bytes 18874372
  229.0 1.8 copy-start.24
  230.8 4.6 copy-start.42
  252.1 2.7 slice-start
  252.8 2.5 slice-start.1
  266.1 32.4 %all-to-all-start.4 = ((bf16[4,2,73728]{2,1,0:T(2,128)(2,1)}), bf16[4,2,73728]{2,1,0:T(2,128)(2,1)}, u32[]{:S(2)}, u32[]{:S(2)}) async-start(bf16[4,2,73728]{2,1,0:T(2,128)(2,1)} %reshape.772), calls=%async_computation.5 | async-start | bytes 2359296 | tf_op jit(solution)/shard_map/all_to_all | solution.py:70
  270.5 4.6 copy-start.5
  270.5 108.8 %reduce-scatter.7.cloned.1.call-start = ((), (), s32[]{:S(2)}) async-start(), calls=%async_computation.13 | async-start | bytes 1179648 | tf_op jit(solution)/shard_map/reduce_scatter | solution.py:74
  275.1 110.6 %reduce-scatter.13.cloned.1.call-start = ((), (), s32[]{:S(2)}) async-start(), calls=%async_computation.18 | async-start | bytes 245760
  305.7 3.1 copy-start.26
  308.7 1.5 copy-start.3
  308.7 2.7 copy-start.15
  308.7 2.7 copy-start.16
  308.7 2.7 copy-start.28
  308.7 2.7 copy-start.31
  308.7 2.7 copy-start.34
  309.1 1.0 copy-start.13
  311.4 3.0 copy-start.44
  311.4 3.0 copy-start.45
  314.4 23.7 %copy-start.10 = (pred[512,1024]{1,0:T(8,128)(4,1)S(1)}, pred[512,1024]{1,0:T(8,128)(4,1)}, u32[]{:S(2)}) copy-start(pred[512,1024]{1,0:T(8,128)(4,1)} %copy-done.9) | copy-start | bytes 1572868
  314.4 23.7 %copy-start.12 = (bf16[1,1024,3,3,64]{1,4,3,2,0:T(8,128)(2,1)S(1)}, bf16[1,1024,3,3,64]{1,4,3,2,0:T(8,128)(2,1)}, u32[]{:S(2)}) copy-start(bf16[1,1024,3,3,64]{1,4,3,2,0:T(8,128)(2,1)} %copy-done.11) | copy-start | bytes 3538948
  314.4 23.7 %copy-start.37 = (f32[3,512]{1,0:T(4,128)S(1)}, f32[3,512]{1,0:T(4,128)}, u32[]{:S(2)}) copy-start(f32[3,512]{1,0:T(4,128)} %copy-done.36) | copy-start | bytes 18436
  314.4 23.7 %copy-start.39 = (f32[3,512]{1,0:T(4,128)S(1)}, f32[3,512]{1,0:T(4,128)}, u32[]{:S(2)}) copy-start(f32[3,512]{1,0:T(4,128)} %copy-done.38) | copy-start | bytes 18436
  315.3 150.9 %all-gather.16.cloned.1.call-start = ((), (), s32[]{:S(2)}) async-start(), calls=%async_computation.17 | async-start | bytes 5898240 | tf_op jit(solution)/shard_map/all_gather | solution.py:313
  337.9 5.0 copy-start.8
  338.0 5.0 copy-start.41
  338.0 5.0 copy-start.43
  338.0 186.5 %reduce-scatter.11.cloned.1.call-start = ((), (), s32[]{:S(2)}) async-start(), calls=%async_computation.15 | async-start | bytes 5898240 | tf_op jit(solution)/shard_map/reduce_scatter | solution.py:282
  350.1 21.6 %copy-start.14 = (bf16[256,3,12,64]{0,3,2,1:T(8,128)(2,1)S(1)}, bf16[256,3,12,64]{0,3,2,1:T(8,128)(2,1)}, u32[]{:S(2)}) copy-start(bf16[256,3,12,64]{0,3,2,1:T(8,128)(2,1)} %copy-done.13) | copy-start | bytes 3538948
  350.1 21.7 %copy-start.29 = (f32[256]{0:T(256)S(1)}, f32[256]{0:T(256)}, u32[]{:S(2)}) copy-start(f32[256]{0:T(256)} %copy-done.27) | copy-start | bytes 3076
  350.1 21.7 %copy-start.35 = (f32[256]{0:T(256)S(1)}, f32[256]{0:T(256)}, u32[]{:S(2)}) copy-start(f32[256]{0:T(256)} %copy-done.33) | copy-start | bytes 3076
  370.5 0.7 copy-start.17
  375.9 3.4 copy-start.18
  375.9 3.4 copy-start.19
  375.9 8.4 %copy-start.23 = (f32[256,768]{1,0:T(8,128)S(1)}, f32[256,768]{1,0:T(8,128)}, u32[]{:S(2)}) copy-start(f32[256,768]{1,0:T(8,128)} %get-tuple-element.100) | copy-start | bytes 2359300
  375.9 8.4 %copy-start.32 = (f32[768]{0:T(1024)S(1)}, f32[768]{0:T(1024)}, u32[]{:S(2)}) copy-start(f32[768]{0:T(1024)} %copy-done.30) | copy-start | bytes 9220
  376.0 210.8 %all-reduce.13.cloned.1.call-start = ((), (), s32[]{:S(2)}) async-start(), calls=%async_computation.16 | async-start | bytes 2359296 | tf_op jit(solution)/shard_map/psum | solution.py:309
  526.4 3.0 copy-start.6
Sparse Core Ops, SparseCore 0:
  9.8 30.3 all-gather.9
  42.1 37.3 all-gather.11
  81.3 37.3 all-gather.13
  120.4 47.2 all-gather.7
  199.4 8.5 reduce-scatter.8
  222.1 112.6 all-reduce.14
  337.6 8.1 reduce-scatter.6
  348.6 25.4 reduce-scatter.12
  376.2 89.9 all-gather.15
  469.0 55.3 reduce-scatter.10
  526.8 59.8 all-reduce.12
